TPU v7x, 32 devices: a whole 2x2x4 slice. The times are simulated.
32 devices in a mesh: grp: 2 (over y), row: 4 (over z), col: 2 (over x), sub: 2 (over core).
Axes of the slice: x: 2, y: 2, z: 4, core: 2. Of those that a mesh axis runs over, the one named last changes fastest.
Arguments:
- spectra: bfloat16 [128, 3, 2, 256], P(('grp', 'row', 'col', 'sub')), parts along dimension 0, may hold values from -24 to 24
- valid_mask: int32 [128, 3], P(('grp', 'row', 'col', 'sub')), parts along dimension 0, may hold values 0 or 1
Outputs:
- maxima: float32 [4, 128, 16], P(('col', 'sub'), ('grp', 'row')), parts along dimension 1
There are 2 independent parts, one for each index of `grp`. A program takes and returns all parts, laid end to end along the dimension named above; each array names one. Nothing has to cross between parts.
All inputs are finite; a program needn't handle non-finite values. No bound on the sum of `valid_mask` on one device may be relied on, other than what follows from the above.
Results may differ from a plain program's by a relative error of at most 0.0003.
Values may be sent and summed in bfloat16 or wider, within the bound.
No kernel may reach another device: no remote copies, remote signals or barrier semaphores. Data moves between devices by JAX's collectives and lax.ppermute only.
A program may use at most 64 MiB of HBM per device.

v0:
```python
import math

import jax
import jax.numpy as jnp
from jax import lax
from jax.sharding import PartitionSpec as P

BINS = 256
NSAMP = 2048
FIRST_BIN = 20
MAXLAG = 32


FLOOR = 0.25


def phase_tables():
    lag_values = jnp.arange(-MAXLAG, MAXLAG + 1).astype(jnp.float32)
    frequency = (FIRST_BIN + jnp.arange(BINS)).astype(jnp.float32)
    angle = 2.0 * math.pi / NSAMP * lag_values[:, None] * frequency[None, :]
    return (jnp.cos(angle), jnp.sin(angle))


def masked_of(records, flags):
    return records * flags.astype(jnp.bfloat16)[:, :, None, None]


def energy_of(masked):
    floats = masked.astype(jnp.float32)
    return jnp.mean(floats * floats, axis=(2, 3))


def rotate(masked, cosine, sine):
    floats = masked.astype(jnp.float32)
    real_part = floats[:, None, :, 0, :]
    imag_part = floats[:, None, :, 1, :]
    cos_table = cosine[None, :, None, :]
    sin_table = sine[None, :, None, :]
    new_real = real_part * cos_table - imag_part * sin_table
    new_imag = real_part * sin_table + imag_part * cos_table
    stacked = jnp.stack([new_real, new_imag], axis=3)
    return stacked.reshape(masked.shape[0] * cosine.shape[0], -1)


def pair_values(rotated, row_energy, row_flags, col_masked, col_flags):
    row_count = row_energy.shape[0]
    col_count = col_masked.shape[0]
    bin_count = col_masked.shape[3]
    flat_cols = col_masked.reshape(col_count, -1).astype(jnp.float32)
    products = lax.dot_general(
        rotated,
        flat_cols,
        (((1,), (1,)), ((), ())),
        precision=lax.Precision.HIGHEST,
        preferred_element_type=jnp.float32,
    )
    peak_value = jnp.max(products.reshape(row_count, -1, col_count), axis=1) / (2.0 * bin_count)
    col_energy = energy_of(col_masked)
    shared_row = jnp.sum((row_energy * row_flags)[:, None, :] * col_flags[None, :, :], axis=2)
    shared_col = jnp.sum(row_flags[:, None, :] * (col_energy * col_flags)[None, :, :], axis=2)
    return peak_value / jnp.sqrt(jnp.maximum(shared_row * shared_col, FLOOR))


def merge_mirror(pair_grid, own_blocks, received, shard_rows):
    mirrored = received.transpose(1, 3, 0, 2).reshape(pair_grid.shape)
    keep_cols = jnp.repeat(own_blocks, shard_rows)[None, :]
    return jnp.where(keep_cols, pair_grid, mirrored)


def shards(spectra, valid_mask):
    shard_rows = spectra.shape[0]
    row_total = lax.axis_size("row")
    row_index = lax.axis_index("row")
    cosine, sine = phase_tables()
    row_spec, row_mask = (
        lax.all_gather(spectra, ("col", "sub"), axis=0, tiled=True),
        lax.all_gather(valid_mask, ("col", "sub"), axis=0, tiled=True),
    )
    row_masked = masked_of(row_spec, row_mask)
    row_energy = energy_of(row_masked)
    row_flags = row_mask.astype(jnp.float32)
    rotated = rotate(row_masked, cosine, sine)
    block_rows = row_spec.shape[0]
    groups = block_rows // shard_rows
    block_ids = jnp.arange(row_total)

    def values(col_spec, col_mask):
        return pair_values(
            rotated,
            row_energy,
            row_flags,
            masked_of(col_spec, col_mask),
            col_mask.astype(jnp.float32),
        )

    piece = (
        lax.all_gather(spectra, "row", axis=0, tiled=True),
        lax.all_gather(valid_mask, "row", axis=0, tiled=True),
    )
    piece_rows = piece[0].shape[0]
    last_block = (jnp.int32(0) + piece_rows - 1) // shard_rows
    piece_values = lax.cond(
        last_block >= row_index,
        lambda: values(piece[0], piece[1]),
        lambda: jnp.zeros((block_rows, piece_rows), jnp.float32),
    )
    pair_grid = piece_values
    own_blocks = block_ids >= row_index
    outgoing = pair_grid.reshape(groups, shard_rows, row_total, shard_rows).transpose(2, 0, 1, 3)
    received = lax.all_to_all(
        lax.all_to_all(outgoing, "row", split_axis=0, concat_axis=0, tiled=True),
        ("col", "sub"),
        split_axis=1,
        concat_axis=1,
        tiled=True,
    )
    pair_grid = merge_mirror(pair_grid, own_blocks, received, shard_rows)
    return pair_grid[None]


def solution(mesh):
    in_specs = (
        P(("grp", "row", "col", "sub"), None, None, None),
        P(("grp", "row", "col", "sub"), None),
    )
    out_specs = P(("col", "sub"), ("grp", "row"), None)
    return jax.shard_map(shards, mesh=mesh, in_specs=in_specs, out_specs=out_specs, check_vma=False)
```

profile of v0, /device:TPU:0, one launch (start us, length us, event | category | flops | bytes accessed | tf_op | source)
XLA Modules:
  0.0 90.0 jit_solution(2294242378438351198)
XLA Ops:
  0.0 6.3 %all-gather.1 = s32[4,4,3]{2,1,0:T(4,128)S(1)} all-gather(s32[1,4,3]{2,1,0:T(4,128)} %bitcast.23), channel_id=1, replica_groups=mesh['grp'=2,'row'=4,'col'=2,'sub'=2] {'col','sub'}, dimensions={0}, use_global_device_ids=true | all-gather | bytes 240 | tf_op jit(solution)/shard_map/all_gather | solution.py:77
  6.3 12.7 %all-gather = s32[4,4,3]{2,1,0:T(4,128)S(1)} all-gather(s32[1,4,3]{2,1,0:T(4,128)} %bitcast.24), channel_id=1, replica_groups=mesh['grp'=2,'row'=4,'col'=2,'sub'=2] {'row'}, dimensions={0}, use_global_device_ids=true | all-gather | bytes 240 | tf_op jit(solution)/shard_map/all_gather | solution.py:98
  19.0 5.4 %all_gather.14 = bf16[16,3,2,256]{3,2,1,0:T(2,128)(2,1)S(1)} all-gather(bf16[4,3,2,256]{3,2,1,0:T(2,128)(2,1)} %param.4), channel_id=1, replica_groups=mesh['grp'=2,'row'=4,'col'=2,'sub'=2] {'col','sub'}, dimensions={0}, use_global_device_ids=true | all-gather | bytes 61440 | tf_op jit(solution)/shard_map/all_gather | solution.py:76
  24.4 13.3 %all_gather.13 = bf16[16,3,2,256]{3,2,1,0:T(2,128)(2,1)S(1)} all-gather(bf16[4,3,2,256]{3,2,1,0:T(2,128)(2,1)} %param.4), channel_id=1, replica_groups=mesh['grp'=2,'row'=4,'col'=2,'sub'=2] {'row'}, dimensions={0}, use_global_device_ids=true | all-gather | bytes 61440 | tf_op jit(solution)/shard_map/all_gather | solution.py:97
  37.7 0.1 copy.90
  37.8 0.1 reshape.117
  38.1 0.3 multiply_cosine_fusion
  38.4 7.0 %multiply_subtract_fusion = (f32[16,65,3,1,256]{4,3,2,1,0:T(1,128)S(1)}, f32[16,65,3,1,256]{4,3,2,1,0:T(1,128)}) fusion(f32[65,256]{1,0:T(8,128)S(1)} %get-tuple-element.84, f32[16,3,256]{2,1,0:T(4,128)S(1)} %copy.93, f32[65,256]{1,0:T(8,128)S(1)} %get-tuple-element.83, f32[16,3,256]{2,1,0:T(4,128)S(1)} %copy.92), kind=kLoop, calls=%fused_computation.12 | loop fusion | flops 4792320 | bytes 6621184 | tf_op jit(solution)/shard_map/sub | solution.py:39
  45.4 10.5 %pad_maximum_fusion = f32[16,65,3,2,256]{4,3,2,1,0:T(2,128)} fusion(f32[16,65,3,1,256]{4,3,2,1,0:T(1,128)} %get-tuple-element.78, f32[16,65,3,1,256]{4,3,2,1,0:T(1,128)S(1)} %get-tuple-element.77), kind=kLoop, calls=%fused_computation.10 | loop fusion | flops 1597440 | bytes 12779520 | tf_op jit(solution)/shard_map/stack | solution.py:41
  55.9 16.3 %conditional.1 = (f32[16,16]{0,1:T(8,128)S(1)}) conditional(s32[]{:T(128)} %convert_element_type.52, () %tuple.16, (s32[16,3]{1,0:T(8,128)S(1)}, bf16[16,3,2,256]{3,2,1,0:T(2,128)(2,1)S(1)}, f32[16,65,3,2,256]{4,3,2,1,0:T(2,128)}, f32[16,3,2,256]{3,0,2,1:T(8,128)S(1)}, f32[4,4,3]{1,0,2:T(4,128)S(1)}) %tuple.33), branch_computations={%region_0.0_spmd, %region_1.7_spmd} | conditional | flops 306876160 | bytes 19795660 | solution.py:102
  56.0 0.1 copy.97
  56.1 0.4 multiply_reduce_fusion
  57.1 9.1 %reshape.107 = f32[1040,1536]{1,0:T(8,128)} reshape(f32[16,65,3,2,256]{4,3,2,1,0:T(2,128)} %get-tuple-element.37) | data formatting | bytes 12779520 | tf_op jit(solution)/shard_map/reshape | solution.py:42
  66.2 5.8 %convolution_bitcast_fusion = f32[1040,16]{0,1:T(8,128)S(1)} fusion(bf16[16,1536]{1,0:T(8,128)(2,1)S(1)} %reshape.106, f32[1040,1536]{1,0:T(8,128)} %reshape.107), kind=kOutput, calls=%fused_computation | convolution fusion | flops 306708480 | bytes 6505472 | tf_op jit(solution)/shard_map/cond/branch_1_fun/dot_general | solution.py:50
  71.9 0.1 reshape.108
  72.1 0.1 reduce_max.9
  72.3 0.1 reshape.111
  72.4 0.2 copy.99
  72.6 8.9 %all_to_all.10 = f32[4,4,4,4]{2,3,1,0:T(4,128)S(1)} all-to-all(f32[4,4,4,4]{2,3,1,0:T(4,128)S(1)} %copy.99), channel_id=1, replica_groups=mesh['grp'=2,'row'=4,'col'=2,'sub'=2] {'row'}, dimensions={0} | all-to-all | bytes 2048 | tf_op jit(solution)/shard_map/all_to_all | solution.py:111
  81.5 0.6 copy.100
  82.1 3.3 %all-to-all-start.1 = ((f32[4,4,4,4]{2,3,0,1:T(4,128)}), f32[4,4,4,4]{2,3,0,1:T(4,128)S(1)}, u32[]{:S(2)}, u32[]{:S(2)}) async-start(f32[4,4,4,4]{2,3,0,1:T(4,128)} %copy.100), calls=%async_computation.1 | async-start | bytes 65536 | tf_op jit(solution)/shard_map/all_to_all | solution.py:110
  85.4 0.1 broadcast_in_dim.17
  85.5 3.7 %all-to-all-done.1 = f32[4,4,4,4]{2,3,0,1:T(4,128)S(1)} async-done(((f32[4,4,4,4]{2,3,0,1:T(4,128)}), f32[4,4,4,4]{2,3,0,1:T(4,128)S(1)}, u32[]{:S(2)}, u32[]{:S(2)}) %all-to-all-start.1) | async-done | bytes 1056 | tf_op jit(solution)/shard_map/all_to_all | solution.py:110
  89.3 0.6 select_bitcast_fusion
  (25 shorter events, 1.1 us)
Async XLA Ops:
  82.1 7.2 %all-to-all-start.1 = ((f32[4,4,4,4]{2,3,0,1:T(4,128)}), f32[4,4,4,4]{2,3,0,1:T(4,128)S(1)}, u32[]{:S(2)}, u32[]{:S(2)}) async-start(f32[4,4,4,4]{2,3,0,1:T(4,128)} %copy.100), calls=%async_computation.1 | async-start | bytes 65536 | tf_op jit(solution)/shard_map/all_to_all | solution.py:110
where the time goes:
time: 90.4 us; the launch traced here: 90 us
  blocking collectives  46.6 us (52%)
  other arithmetic  19.2 us (21%)
  local copies, waits for them, and re-layouts  11.3 us (12%)
  matrix products  5.75 us (6%)
  waiting for transfers between devices  3.74 us (4%)
  starting transfers between devices  3.26 us (4%)
    all_gather x1, blocking collectives, shards(): lax.all_gather(spectra, 'row', axis=0, tiled=True)  13.3 us
    all_gather x1, blocking collectives, shards(): lax.all_gather(valid_mask, 'row', axis=0, tiled=True)  12.7 us
    another operation x1, other arithmetic, rotate(): stacked = jnp.stack([new_real, new_imag], axis=3)  10.5 us
    reshape x1, local copies, waits for them, and re-layouts, rotate(): return stacked.reshape(masked.shape[0] * cosine.shape[0], -1)  9.08 us
    all_to_all x1, blocking collectives, shards(): lax.all_to_all(outgoing, 'row', split_axis=0, concat_axis=0, tiled=True)  8.9 us
    sub x1, other arithmetic, rotate(): new_real = real_part * cos_table - imag_part * sin_table  6.98 us
    all_gather x1, blocking collectives, shards(): lax.all_gather(valid_mask, ('col', 'sub'), axis=0, tiled=True)  6.27 us
    dot_general x1, matrix products, pair_values(): lax.dot_general(rotated, flat_cols, (((1,), (1,)), ((), ())), precision=l...  5.75 us
  transfers between devices with their start and end apart: 1, of which 1 were waited for; matrix products, arithmetic and copies ran while one was open for 0% of the time, Pallas kernels for 0%

commit v1 on v0

v1 whole, which is shorter than its diff:
```python
import functools
import math

import jax
import jax.numpy as jnp
import numpy as np
from jax import lax
from jax.experimental import pallas as pl
from jax.experimental.pallas import tpu as pltpu
from jax.sharding import PartitionSpec as P

BINS = 256
COMP = 3
NSAMP = 2048
FIRST_BIN = 20
MAXLAG = 32
FLOOR = 0.25
PLANES = 3 * COMP
LAGS = 40


def phase_tables():
    lag = np.arange(LAGS)
    lag = np.where(lag <= MAXLAG, lag, 0)
    angle = 2.0 * math.pi / NSAMP * lag[:, None] * (FIRST_BIN + np.arange(BINS))[None, :]
    both = []
    for table in (np.cos(angle), np.sin(angle)):
        high = table.astype(jnp.bfloat16)
        low = (table - high.astype(np.float64)).astype(jnp.bfloat16)
        both.append(np.concatenate([high, low], axis=0))
    return np.stack(both)


def pack_kernel(spectra_ref, mask_ref, out_ref):
    floats = spectra_ref[...].astype(jnp.float32)
    flags = mask_ref[...].astype(jnp.float32)
    for c in range(COMP):
        flag = jnp.broadcast_to(flags[:, c : c + 1], (flags.shape[0], BINS))
        out_ref[2 * c] = (floats[:, c, 0, :] * flag).astype(jnp.bfloat16)
        out_ref[2 * c + 1] = (floats[:, c, 1, :] * flag).astype(jnp.bfloat16)
        out_ref[2 * COMP + c] = flag.astype(jnp.bfloat16)


def pack(spectra, valid_mask):
    rows = spectra.shape[0]
    return pl.pallas_call(
        pack_kernel,
        out_shape=jax.ShapeDtypeStruct((PLANES, rows, BINS), jnp.bfloat16),
        in_specs=[pl.BlockSpec(memory_space=pltpu.VMEM)] * 2,
        out_specs=pl.BlockSpec(memory_space=pltpu.VMEM),
        compiler_params=pltpu.CompilerParams(vmem_limit_bytes=1 << 20),
        name="pack",
    )(spectra, valid_mask)


def split(value):
    high = value.astype(jnp.bfloat16)
    return high, (value - high.astype(jnp.float32)).astype(jnp.bfloat16)


def dot_nt(left, right):
    return lax.dot_general(left, right, (((1,), (1,)), ((), ())), preferred_element_type=jnp.float32)


def shared_sums(left, right):
    total = None
    for one, other in zip(left, right):
        for i in range(len(one)):
            for j in range(len(other)):
                term = dot_nt(one[i], other[j])
                total = term if total is None else total + term
    return total / (2.0 * BINS)


def pair_kernel(n_cs, n_row, *refs):
    own_ref = refs[0]
    cs_refs = refs[1:n_cs]
    down_refs = refs[n_cs : n_cs + n_row - 1]
    up_refs = refs[n_cs + n_row - 1 : n_cs + 2 * n_row - 2]
    table_ref, out_ref, row_scr, col_scr, x_scr, y_scr = refs[n_cs + 2 * n_row - 2 :]
    shard = own_ref.shape[1]
    me_cs = lax.axis_index("col") * lax.axis_size("sub") + lax.axis_index("sub")
    me_row = lax.axis_index("row")
    own = own_ref[...].astype(jnp.float32)
    row_scr[me_cs] = own
    col_scr[me_row] = own
    for k in range(1, n_cs):
        row_scr[me_cs ^ k] = cs_refs[k - 1][...].astype(jnp.float32)
    for k in range(1, n_row):
        down = down_refs[k - 1][...].astype(jnp.float32)
        up = up_refs[k - 1][...].astype(jnp.float32)
        other = me_row ^ k
        col_scr[other] = jnp.where(other > me_row, down, up)
    rows, cols = n_cs * shard, n_row * shard
    per = 128 // cols
    col_planes = [jnp.concatenate([col_scr[j, q] for j in range(n_row)], axis=0) for q in range(PLANES)]
    for a in range(rows):
        x, y = None, None
        for c in range(COMP):
            re = row_scr[a // shard, 2 * c, pl.ds(a % shard, 1), :]
            im = row_scr[a // shard, 2 * c + 1, pl.ds(a % shard, 1), :]
            xc = re * col_planes[2 * c] + im * col_planes[2 * c + 1]
            yc = im * col_planes[2 * c] - re * col_planes[2 * c + 1]
            x = xc if x is None else x + xc
            y = yc if y is None else y + yc
        place = (a // per * per + (per - a % per) % per) * cols
        x_scr[pl.ds(place, cols), :] = x
        y_scr[pl.ds(place, cols), :] = y
    halves = []
    for scr, i in ((x_scr, 0), (y_scr, 1)):
        high, low = split(scr[...])
        first = dot_nt(table_ref[i], high)
        second = dot_nt(table_ref[i, :LAGS], low)
        halves.append(first[:LAGS] + first[LAGS:] + second)
    best = jnp.max(halves[0] + jnp.abs(halves[1]), axis=0, keepdims=True)
    pieces = []
    for h in range(rows // per):
        piece = jnp.broadcast_to(best[:, 128 * h : 128 * (h + 1)], (per, 128))
        pieces.append(pltpu.roll(piece, 0, 1, stride=cols, stride_axis=0)[:, :cols])
    peak = jnp.concatenate(pieces, axis=0) / (2.0 * BINS)
    row_planes = [jnp.concatenate([row_scr[j, q] for j in range(n_cs)], axis=0) for q in range(PLANES)]

    def energy(planes):
        return [split(planes[2 * c] * planes[2 * c] + planes[2 * c + 1] * planes[2 * c + 1]) for c in range(COMP)]

    def flags(planes):
        return [(planes[2 * COMP + c].astype(jnp.bfloat16),) for c in range(COMP)]

    shared_row = shared_sums(energy(row_planes), flags(col_planes))
    shared_col = shared_sums(flags(row_planes), energy(col_planes))
    out_ref[0] = peak / jnp.sqrt(jnp.maximum(shared_row * shared_col, FLOOR))


def shards_small(spectra, valid_mask):
    n_row = lax.axis_size("row")
    n_cs = lax.axis_size("col") * lax.axis_size("sub")
    shard = spectra.shape[0]
    own = pack(spectra, valid_mask)
    cs_axes = ("col", "sub")
    cs, down, up = {}, {}, {}
    for k in (3, 2, 1):
        up[k] = lax.ppermute(own, "row", [(i, i ^ k) for i in range(n_row) if i < i ^ k])
    for k in (3, 2):
        cs[k] = lax.ppermute(own, cs_axes, [(i, i ^ k) for i in range(n_cs)])
    for k in (1, 2, 3):
        down[k] = lax.ppermute(own, "row", [(i, i ^ k) for i in range(n_row) if i > i ^ k])
    cs[1] = lax.ppermute(own, cs_axes, [(i, i ^ 1) for i in range(n_cs)])
    cs, down, up = ([d[k] for k in (1, 2, 3)] for d in (cs, down, up))
    rows, cols = n_cs * shard, n_row * shard
    return pl.pallas_call(
        functools.partial(pair_kernel, n_cs, n_row),
        out_shape=jax.ShapeDtypeStruct((1, rows, cols), jnp.float32),
        scratch_shapes=[
            pltpu.VMEM((n_cs, PLANES, shard, BINS), jnp.float32),
            pltpu.VMEM((n_row, PLANES, shard, BINS), jnp.float32),
            pltpu.VMEM((rows * cols, BINS), jnp.float32),
            pltpu.VMEM((rows * cols, BINS), jnp.float32),
        ],
        in_specs=[pl.BlockSpec(memory_space=pltpu.VMEM)] * (n_cs + 2 * n_row - 1),
        out_specs=pl.BlockSpec(memory_space=pltpu.VMEM),
        compiler_params=pltpu.CompilerParams(vmem_limit_bytes=8 << 20),
        name="pairs",
    )(own, *cs, *down, *up, jnp.asarray(phase_tables()))


def shards_large(spectra, valid_mask):
    def planes(axes):
        records = lax.all_gather(spectra, axes, axis=0, tiled=True)
        flags = lax.all_gather(valid_mask, axes, axis=0, tiled=True)
        masked = (records * flags.astype(jnp.bfloat16)[:, :, None, None]).astype(jnp.float32)
        return masked, jnp.mean(masked * masked, axis=(2, 3)), flags.astype(jnp.float32)

    row, row_energy, row_flags = planes(("col", "sub"))
    col, col_energy, col_flags = planes("row")
    table = phase_tables().astype(np.float32)
    cosine, sine = table[:, : MAXLAG + 1] + table[:, LAGS : LAGS + MAXLAG + 1]

    def one(args):
        row_one, energy_one, flags_one = args
        re, im = row_one[None, :, 0], row_one[None, :, 1]
        x = jnp.sum(re * col[:, :, 0] + im * col[:, :, 1], axis=1)
        y = jnp.sum(im * col[:, :, 0] - re * col[:, :, 1], axis=1)
        even = jnp.dot(x, cosine.T, precision=lax.Precision.HIGHEST)
        odd = jnp.dot(y, sine.T, precision=lax.Precision.HIGHEST)
        peak = jnp.max(even + jnp.abs(odd), axis=1) / (2.0 * BINS)
        shared_row = jnp.sum((energy_one * flags_one)[None] * col_flags, axis=1)
        shared_col = jnp.sum(flags_one[None] * (col_energy * col_flags), axis=1)
        return peak / jnp.sqrt(jnp.maximum(shared_row * shared_col, FLOOR))

    return lax.map(one, (row, row_energy, row_flags))[None]


def solution(mesh):
    small = mesh.shape["row"] == 4 and mesh.shape["col"] == 2 and mesh.shape["sub"] == 2
    in_specs = (
        P(("grp", "row", "col", "sub"), None, None, None),
        P(("grp", "row", "col", "sub"), None),
    )
    out_specs = P(("col", "sub"), ("grp", "row"), None)
    return jax.shard_map(
        shards_small if small else shards_large, mesh=mesh, in_specs=in_specs, out_specs=out_specs, check_vma=False
    )
```

time: 90.4 us -> 23.5 us (0.26)
  the two profiles are of different devices: /device:TPU:0 before, /device:TPU:25 now
where the time goes in v1:
time: 23.5 us; the launch traced here: 23.1 us
  starting transfers between devices  17.5 us (74%)
  local copies, waits for them, and re-layouts  2.28 us (10%)
  waiting for transfers between devices  2.14 us (9%)
  Pallas kernels  1.19 us (5%)
    ppermute x3, starting transfers between devices, shards_small(): lax.ppermute(own, 'row', [(i, i ^ k) for i in range(n_row) if i > i ^ k])  10.2 us
    ppermute x3, starting transfers between devices, shards_small(): lax.ppermute(own, 'row', [(i, i ^ k) for i in range(n_row) if i < i ^ k])  3.86 us
    ppermute x2, starting transfers between devices, shards_small(): cs[k] = lax.ppermute(own, cs_axes, [(i, i ^ k) for i in range(n_cs)])  3.21 us
    unnamed x6, local copies, waits for them, and re-layouts  2.28 us
    ppermute x2, waiting for transfers between devices, shards_small(): cs[k] = lax.ppermute(own, cs_axes, [(i, i ^ k) for i in range(n_cs)])  2.12 us
    pallas_call x1, Pallas kernels, shards_small(): pl.pallas_call(functools.partial(pair_kernel, n_cs, n_row), out_shape=jax...  1.11 us
  transfers between devices with their start and end apart: 9, of which 2 were waited for; matrix products, arithmetic and copies ran while one was open for 0% of the time, Pallas kernels for 0%

profile of v1, /device:TPU:25, one launch (start us, length us, event | category | flops | bytes accessed | tf_op | source)
XLA Modules:
  0.0 23.1 jit_solution(7613962012762639818)
XLA Ops:
  0.0 0.0 copy-start.1
  0.0 0.7 %copy-done.1 = bf16[4,3,2,256]{3,2,1,0:T(2,128)(2,1)S(1)} copy-done((bf16[4,3,2,256]{3,2,1,0:T(2,128)(2,1)S(1)}, bf16[4,3,2,256]{3,2,1,0:T(2,128)(2,1)}, u32[]{:S(2)}) %copy-start.1) | copy-done | bytes 12312
  0.7 0.7 %copy-done.2 = s32[4,3]{1,0:T(4,128)S(1)} copy-done((s32[4,3]{1,0:T(4,128)S(1)}, s32[4,3]{1,0:T(4,128)}, u32[]{:S(2)}) %copy-start.2) | copy-done | bytes 72
  1.4 0.1 pack.1.refs_0_
  1.5 1.3 %collective-permute-start.8 = (bf16[9,4,256]{2,1,0:T(4,128)(2,1)S(1)}, bf16[9,4,256]{2,1,0:T(4,128)(2,1)S(1)}, u32[]{:S(2)}, u32[]{:S(2)}) collective-permute-start(bf16[9,4,256]{2,1,0:T(4,128)(2,1)S(1)} %pack.1.refs_0_), channel_id=1, source_target_pairs={{0,12},{4,8},{1,13},{5,9},{2,14},{6,10},{3,15},{7,11},{16,28},{20,... | collective-permute-start | bytes 55304 | tf_op jit(solution)/shard_map/ppermute | solution.py:142
  2.8 1.3 %collective-permute-start.7 = (bf16[9,4,256]{2,1,0:T(4,128)(2,1)S(1)}, bf16[9,4,256]{2,1,0:T(4,128)(2,1)S(1)}, u32[]{:S(2)}, u32[]{:S(2)}) collective-permute-start(bf16[9,4,256]{2,1,0:T(4,128)(2,1)S(1)} %pack.1.refs_0_), channel_id=1, source_target_pairs={{0,8},{4,12},{1,9},{5,13},{2,10},{6,14},{3,11},{7,15},{16,24},{20,... | collective-permute-start | bytes 55304 | tf_op jit(solution)/shard_map/ppermute | solution.py:142
  4.1 1.3 %collective-permute-start.6 = (bf16[9,4,256]{2,1,0:T(4,128)(2,1)S(1)}, bf16[9,4,256]{2,1,0:T(4,128)(2,1)S(1)}, u32[]{:S(2)}, u32[]{:S(2)}) collective-permute-start(bf16[9,4,256]{2,1,0:T(4,128)(2,1)S(1)} %pack.1.refs_0_), channel_id=1, source_target_pairs={{0,4},{8,12},{1,5},{9,13},{2,6},{10,14},{3,7},{11,15},{16,20},{24,... | collective-permute-start | bytes 55304 | tf_op jit(solution)/shard_map/ppermute | solution.py:142
  5.4 6.7 %collective-permute-start.5 = (bf16[9,4,256]{2,1,0:T(4,128)(2,1)S(1)}, bf16[9,4,256]{2,1,0:T(4,128)(2,1)S(1)}, u32[]{:S(2)}, u32[]{:S(2)}) collective-permute-start(bf16[9,4,256]{2,1,0:T(4,128)(2,1)S(1)} %pack.1.refs_0_), channel_id=1, source_target_pairs={{8,4},{12,0},{9,5},{13,1},{10,6},{14,2},{11,7},{15,3},{24,20},{28,... | collective-permute-start | bytes 55304 | tf_op jit(solution)/shard_map/ppermute | solution.py:146
  12.0 1.3 %collective-permute-start.4 = (bf16[9,4,256]{2,1,0:T(4,128)(2,1)S(1)}, bf16[9,4,256]{2,1,0:T(4,128)(2,1)S(1)}, u32[]{:S(2)}, u32[]{:S(2)}) collective-permute-start(bf16[9,4,256]{2,1,0:T(4,128)(2,1)S(1)} %pack.1.refs_0_), channel_id=1, source_target_pairs={{8,0},{12,4},{9,1},{13,5},{10,2},{14,6},{11,3},{15,7},{24,16},{28,... | collective-permute-start | bytes 55304 | tf_op jit(solution)/shard_map/ppermute | solution.py:146
  13.3 0.0 collective-permute-done.8.refs_9_
  13.4 2.2 %collective-permute-start.3 = (bf16[9,4,256]{2,1,0:T(4,128)(2,1)S(1)}, bf16[9,4,256]{2,1,0:T(4,128)(2,1)S(1)}, u32[]{:S(2)}, u32[]{:S(2)}) collective-permute-start(bf16[9,4,256]{2,1,0:T(4,128)(2,1)S(1)} %pack.1.refs_0_), channel_id=1, source_target_pairs={{4,0},{12,8},{5,1},{13,9},{6,2},{14,10},{7,3},{15,11},{20,16},{28,... | collective-permute-start | bytes 55304 | tf_op jit(solution)/shard_map/ppermute | solution.py:146
  15.5 0.0 collective-permute-done.7.refs_8_
  15.6 3.0 %collective-permute-start.2 = (bf16[9,4,256]{2,1,0:T(4,128)(2,1)S(1)}, bf16[9,4,256]{2,1,0:T(4,128)(2,1)S(1)}, u32[]{:S(2)}, u32[]{:S(2)}) collective-permute-start(bf16[9,4,256]{2,1,0:T(4,128)(2,1)S(1)} %pack.1.refs_0_), channel_id=1, source_target_pairs={{0,3},{1,2},{2,1},{3,0},{4,7},{5,6},{6,5},{7,4},{8,11},{9,10},{10,... | collective-permute-start | bytes 55304 | tf_op jit(solution)/shard_map/ppermute | solution.py:144
  18.5 0.0 collective-permute-done.6.refs_7_
  18.5 0.3 %collective-permute-start.1 = (bf16[9,4,256]{2,1,0:T(4,128)(2,1)S(1)}, bf16[9,4,256]{2,1,0:T(4,128)(2,1)S(1)}, u32[]{:S(2)}, u32[]{:S(2)}) collective-permute-start(bf16[9,4,256]{2,1,0:T(4,128)(2,1)S(1)} %pack.1.refs_0_), channel_id=1, source_target_pairs={{0,2},{1,3},{2,0},{3,1},{4,6},{5,7},{6,4},{7,5},{8,10},{9,11},{10,... | collective-permute-start | bytes 55304 | tf_op jit(solution)/shard_map/ppermute | solution.py:144
  18.8 0.0 collective-permute-done.5.refs_6_
  18.8 0.2 collective-permute-start
  19.0 0.0 collective-permute-done.4.refs_5_
  19.0 0.0 collective-permute-done.3.refs_4_
  19.0 1.3 %collective-permute-done.2.refs_3_ = bf16[9,4,256]{2,1,0:T(4,128)(2,1)S(1)} collective-permute-done((bf16[9,4,256]{2,1,0:T(4,128)(2,1)S(1)}, bf16[9,4,256]{2,1,0:T(4,128)(2,1)S(1)}, u32[]{:S(2)}, u32[]{:S(2)}) %collective-permute-start.2) | collective-permute-done | bytes 18464 | tf_op jit(solution)/shard_map/ppermute | solution.py:144
  20.4 0.8 %collective-permute-done.1.refs_2_ = bf16[9,4,256]{2,1,0:T(4,128)(2,1)S(1)} collective-permute-done((bf16[9,4,256]{2,1,0:T(4,128)(2,1)S(1)}, bf16[9,4,256]{2,1,0:T(4,128)(2,1)S(1)}, u32[]{:S(2)}, u32[]{:S(2)}) %collective-permute-start.1) | collective-permute-done | bytes 18464 | tf_op jit(solution)/shard_map/ppermute | solution.py:144
  21.1 0.0 collective-permute-done.refs_1_
  21.1 0.9 %copy-done = bf16[2,80,256]{2,1,0:T(8,128)(2,1)S(1)} copy-done((bf16[2,80,256]{2,1,0:T(8,128)(2,1)S(1)}, bf16[2,80,256]{2,1,0:T(8,128)(2,1)}, u32[]{:S(2)}) %copy-start) | copy-done | bytes 81944
  22.0 1.1 %pairs.1 = f32[1,16,16]{2,1,0:T(8,128)} custom-call(bf16[9,4,256]{2,1,0:T(4,128)(2,1)S(1)} %pack.1.refs_0_, bf16[9,4,256]{2,1,0:T(4,128)(2,1)S(1)} %collective-permute-done.refs_1_, bf16[9,4,256]{2,1,0:T(4,128)(2,1)S(1)} %collective-permute-done.1.refs_2_, bf16[9,4,256]{2,1,0:T(4,128)(2,1)S(1)} %collective-permute-done.2.refs_3_, ...), custom_call_target="tpu_custom_call" | custom-call | tf_op jit(solution)/shard_map/pairs/pallas_call | solution.py:150
  (2 shorter events, 0.0 us)
Async XLA Ops:
  0.0 0.7 %copy-start.1 = (bf16[4,3,2,256]{3,2,1,0:T(2,128)(2,1)S(1)}, bf16[4,3,2,256]{3,2,1,0:T(2,128)(2,1)}, u32[]{:S(2)}) copy-start(bf16[4,3,2,256]{3,2,1,0:T(2,128)(2,1)} %spectra_ref.1) | copy-start | bytes 36868
  0.7 0.7 %copy-start.2 = (s32[4,3]{1,0:T(4,128)S(1)}, s32[4,3]{1,0:T(4,128)}, u32[]{:S(2)}) copy-start(s32[4,3]{1,0:T(4,128)} %mask_ref.1) | copy-start | bytes 148
  1.5 11.9 %collective-permute-start.8 = (bf16[9,4,256]{2,1,0:T(4,128)(2,1)S(1)}, bf16[9,4,256]{2,1,0:T(4,128)(2,1)S(1)}, u32[]{:S(2)}, u32[]{:S(2)}) collective-permute-start(bf16[9,4,256]{2,1,0:T(4,128)(2,1)S(1)} %pack.1.refs_0_), channel_id=1, source_target_pairs={{0,12},{4,8},{1,13},{5,9},{2,14},{6,10},{3,15},{7,11},{16,28},{20,... | collective-permute-start | bytes 55304 | tf_op jit(solution)/shard_map/ppermute | solution.py:142
  2.8 12.8 %collective-permute-start.7 = (bf16[9,4,256]{2,1,0:T(4,128)(2,1)S(1)}, bf16[9,4,256]{2,1,0:T(4,128)(2,1)S(1)}, u32[]{:S(2)}, u32[]{:S(2)}) collective-permute-start(bf16[9,4,256]{2,1,0:T(4,128)(2,1)S(1)} %pack.1.refs_0_), channel_id=1, source_target_pairs={{0,8},{4,12},{1,9},{5,13},{2,10},{6,14},{3,11},{7,15},{16,24},{20,... | collective-permute-start | bytes 55304 | tf_op jit(solution)/shard_map/ppermute | solution.py:142
  4.1 14.5 %collective-permute-start.6 = (bf16[9,4,256]{2,1,0:T(4,128)(2,1)S(1)}, bf16[9,4,256]{2,1,0:T(4,128)(2,1)S(1)}, u32[]{:S(2)}, u32[]{:S(2)}) collective-permute-start(bf16[9,4,256]{2,1,0:T(4,128)(2,1)S(1)} %pack.1.refs_0_), channel_id=1, source_target_pairs={{0,4},{8,12},{1,5},{9,13},{2,6},{10,14},{3,7},{11,15},{16,20},{24,... | collective-permute-start | bytes 55304 | tf_op jit(solution)/shard_map/ppermute | solution.py:142
  5.4 13.4 %collective-permute-start.5 = (bf16[9,4,256]{2,1,0:T(4,128)(2,1)S(1)}, bf16[9,4,256]{2,1,0:T(4,128)(2,1)S(1)}, u32[]{:S(2)}, u32[]{:S(2)}) collective-permute-start(bf16[9,4,256]{2,1,0:T(4,128)(2,1)S(1)} %pack.1.refs_0_), channel_id=1, source_target_pairs={{8,4},{12,0},{9,5},{13,1},{10,6},{14,2},{11,7},{15,3},{24,20},{28,... | collective-permute-start | bytes 55304 | tf_op jit(solution)/shard_map/ppermute | solution.py:146
  12.0 7.0 %collective-permute-start.4 = (bf16[9,4,256]{2,1,0:T(4,128)(2,1)S(1)}, bf16[9,4,256]{2,1,0:T(4,128)(2,1)S(1)}, u32[]{:S(2)}, u32[]{:S(2)}) collective-permute-start(bf16[9,4,256]{2,1,0:T(4,128)(2,1)S(1)} %pack.1.refs_0_), channel_id=1, source_target_pairs={{8,0},{12,4},{9,1},{13,5},{10,2},{14,6},{11,3},{15,7},{24,16},{28,... | collective-permute-start | bytes 55304 | tf_op jit(solution)/shard_map/ppermute | solution.py:146
  13.4 5.7 %collective-permute-start.3 = (bf16[9,4,256]{2,1,0:T(4,128)(2,1)S(1)}, bf16[9,4,256]{2,1,0:T(4,128)(2,1)S(1)}, u32[]{:S(2)}, u32[]{:S(2)}) collective-permute-start(bf16[9,4,256]{2,1,0:T(4,128)(2,1)S(1)} %pack.1.refs_0_), channel_id=1, source_target_pairs={{4,0},{12,8},{5,1},{13,9},{6,2},{14,10},{7,3},{15,11},{20,16},{28,... | collective-permute-start | bytes 55304 | tf_op jit(solution)/shard_map/ppermute | solution.py:146
  15.6 4.8 %collective-permute-start.2 = (bf16[9,4,256]{2,1,0:T(4,128)(2,1)S(1)}, bf16[9,4,256]{2,1,0:T(4,128)(2,1)S(1)}, u32[]{:S(2)}, u32[]{:S(2)}) collective-permute-start(bf16[9,4,256]{2,1,0:T(4,128)(2,1)S(1)} %pack.1.refs_0_), channel_id=1, source_target_pairs={{0,3},{1,2},{2,1},{3,0},{4,7},{5,6},{6,5},{7,4},{8,11},{9,10},{10,... | collective-permute-start | bytes 55304 | tf_op jit(solution)/shard_map/ppermute | solution.py:144
  18.5 2.6 %collective-permute-start.1 = (bf16[9,4,256]{2,1,0:T(4,128)(2,1)S(1)}, bf16[9,4,256]{2,1,0:T(4,128)(2,1)S(1)}, u32[]{:S(2)}, u32[]{:S(2)}) collective-permute-start(bf16[9,4,256]{2,1,0:T(4,128)(2,1)S(1)} %pack.1.refs_0_), channel_id=1, source_target_pairs={{0,2},{1,3},{2,0},{3,1},{4,6},{5,7},{6,4},{7,5},{8,10},{9,11},{10,... | collective-permute-start | bytes 55304 | tf_op jit(solution)/shard_map/ppermute | solution.py:144
  18.8 2.4 %collective-permute-start = (bf16[9,4,256]{2,1,0:T(4,128)(2,1)S(1)}, bf16[9,4,256]{2,1,0:T(4,128)(2,1)S(1)}, u32[]{:S(2)}, u32[]{:S(2)}) collective-permute-start(bf16[9,4,256]{2,1,0:T(4,128)(2,1)S(1)} %pack.1.refs_0_), channel_id=1, source_target_pairs={{0,1},{1,0},{2,3},{3,2},{4,5},{5,4},{6,7},{7,6},{8,9},{9,8},{10,11... | collective-permute-start | bytes 55304 | tf_op jit(solution)/shard_map/ppermute | solution.py:147
  21.1 0.9 %copy-start = (bf16[2,80,256]{2,1,0:T(8,128)(2,1)S(1)}, bf16[2,80,256]{2,1,0:T(8,128)(2,1)}, u32[]{:S(2)}) copy-start(bf16[2,80,256]{2,1,0:T(8,128)(2,1)} %constant.2.clone.refs_10_) | copy-start | bytes 245764

commit v2 on v1

--- a/solution.py
+++ b/solution.py
@@ -15,6 +15,8 @@
 FIRST_BIN = 20
 MAXLAG = 32
 FLOOR = 0.25
+CS = ("col", "sub")
+ORDER = (("row", 3), ("row", 2), ("row", 1), (CS, 3), (CS, 2), (CS, 1))
 PLANES = 3 * COMP
 LAGS = 40
 
@@ -31,7 +33,20 @@
     return np.stack(both)
 
 
-def pack_kernel(spectra_ref, mask_ref, out_ref):
+def in_hbm(value):
+    return pltpu.with_memory_space_constraint(value, pltpu.HBM)
+
+
+def pack_kernel(spectra_hbm, mask_hbm, table_hbm, out_ref, table_ref, spectra_ref, mask_ref, sem):
+    copies = [
+        pltpu.make_async_copy(spectra_hbm, spectra_ref, sem.at[0]),
+        pltpu.make_async_copy(mask_hbm, mask_ref, sem.at[1]),
+        pltpu.make_async_copy(table_hbm, table_ref, sem.at[2]),
+    ]
+    for copy in copies:
+        copy.start()
+    copies[0].wait()
+    copies[1].wait()
     floats = spectra_ref[...].astype(jnp.float32)
     flags = mask_ref[...].astype(jnp.float32)
     for c in range(COMP):
@@ -39,18 +54,24 @@
         out_ref[2 * c] = (floats[:, c, 0, :] * flag).astype(jnp.bfloat16)
         out_ref[2 * c + 1] = (floats[:, c, 1, :] * flag).astype(jnp.bfloat16)
         out_ref[2 * COMP + c] = flag.astype(jnp.bfloat16)
-
-
-def pack(spectra, valid_mask):
-    rows = spectra.shape[0]
+    copies[2].wait()
+
+
+def pack(spectra, valid_mask, table):
+    shape = (PLANES, spectra.shape[0], BINS)
     return pl.pallas_call(
         pack_kernel,
-        out_shape=jax.ShapeDtypeStruct((PLANES, rows, BINS), jnp.bfloat16),
-        in_specs=[pl.BlockSpec(memory_space=pltpu.VMEM)] * 2,
-        out_specs=pl.BlockSpec(memory_space=pltpu.VMEM),
+        out_shape=(jax.ShapeDtypeStruct(shape, jnp.bfloat16), jax.ShapeDtypeStruct(table.shape, table.dtype)),
+        in_specs=[pl.BlockSpec(memory_space=pltpu.HBM)] * 3,
+        out_specs=(pl.BlockSpec(memory_space=pltpu.VMEM), pl.BlockSpec(memory_space=pltpu.VMEM)),
+        scratch_shapes=[
+            pltpu.VMEM(spectra.shape, spectra.dtype),
+            pltpu.VMEM(valid_mask.shape, valid_mask.dtype),
+            pltpu.SemaphoreType.DMA((3,)),
+        ],
         compiler_params=pltpu.CompilerParams(vmem_limit_bytes=1 << 20),
         name="pack",
-    )(spectra, valid_mask)
+    )(in_hbm(spectra), in_hbm(valid_mask), in_hbm(table))
 
 
 def split(value):
@@ -74,10 +95,8 @@
 
 def pair_kernel(n_cs, n_row, *refs):
     own_ref = refs[0]
-    cs_refs = refs[1:n_cs]
-    down_refs = refs[n_cs : n_cs + n_row - 1]
-    up_refs = refs[n_cs + n_row - 1 : n_cs + 2 * n_row - 2]
-    table_ref, out_ref, row_scr, col_scr, x_scr, y_scr = refs[n_cs + 2 * n_row - 2 :]
+    moved = dict(zip(reversed(ORDER), refs[1:]))
+    table_ref, out_ref, row_scr, col_scr, x_scr, y_scr = refs[n_cs + n_row - 1 :]
     shard = own_ref.shape[1]
     me_cs = lax.axis_index("col") * lax.axis_size("sub") + lax.axis_index("sub")
     me_row = lax.axis_index("row")
@@ -85,12 +104,9 @@
     row_scr[me_cs] = own
     col_scr[me_row] = own
     for k in range(1, n_cs):
-        row_scr[me_cs ^ k] = cs_refs[k - 1][...].astype(jnp.float32)
+        row_scr[me_cs ^ k] = moved[CS, k][...].astype(jnp.float32)
     for k in range(1, n_row):
-        down = down_refs[k - 1][...].astype(jnp.float32)
-        up = up_refs[k - 1][...].astype(jnp.float32)
-        other = me_row ^ k
-        col_scr[other] = jnp.where(other > me_row, down, up)
+        col_scr[me_row ^ k] = moved["row", k][...].astype(jnp.float32)
     rows, cols = n_cs * shard, n_row * shard
     per = 128 // cols
     col_planes = [jnp.concatenate([col_scr[j, q] for j in range(n_row)], axis=0) for q in range(PLANES)]
@@ -135,17 +151,12 @@
     n_row = lax.axis_size("row")
     n_cs = lax.axis_size("col") * lax.axis_size("sub")
     shard = spectra.shape[0]
-    own = pack(spectra, valid_mask)
-    cs_axes = ("col", "sub")
-    cs, down, up = {}, {}, {}
-    for k in (3, 2, 1):
-        up[k] = lax.ppermute(own, "row", [(i, i ^ k) for i in range(n_row) if i < i ^ k])
-    for k in (3, 2):
-        cs[k] = lax.ppermute(own, cs_axes, [(i, i ^ k) for i in range(n_cs)])
-    for k in (1, 2, 3):
-        down[k] = lax.ppermute(own, "row", [(i, i ^ k) for i in range(n_row) if i > i ^ k])
-    cs[1] = lax.ppermute(own, cs_axes, [(i, i ^ 1) for i in range(n_cs)])
-    cs, down, up = ([d[k] for k in (1, 2, 3)] for d in (cs, down, up))
+    own, table = pack(spectra, valid_mask, jnp.asarray(phase_tables()))
+    moved = {}
+    for axes, k in ORDER:
+        size = n_row if axes == "row" else n_cs
+        moved[axes, k] = lax.ppermute(own, axes, [(i, i ^ k) for i in range(size)])
+    others = [moved[key] for key in reversed(ORDER)]
     rows, cols = n_cs * shard, n_row * shard
     return pl.pallas_call(
         functools.partial(pair_kernel, n_cs, n_row),
@@ -156,11 +167,11 @@
             pltpu.VMEM((rows * cols, BINS), jnp.float32),
             pltpu.VMEM((rows * cols, BINS), jnp.float32),
         ],
-        in_specs=[pl.BlockSpec(memory_space=pltpu.VMEM)] * (n_cs + 2 * n_row - 1),
+        in_specs=[pl.BlockSpec(memory_space=pltpu.VMEM)] * (n_cs + n_row),
         out_specs=pl.BlockSpec(memory_space=pltpu.VMEM),
         compiler_params=pltpu.CompilerParams(vmem_limit_bytes=8 << 20),
         name="pairs",
-    )(own, *cs, *down, *up, jnp.asarray(phase_tables()))
+    )(own, *others, table)
 
 
 def shards_large(spectra, valid_mask):

time: 23.5 us -> 12.2 us (0.52)
  the two profiles are of different devices: /device:TPU:25 before, /device:TPU:0 now
where the time goes in v2:
time: 12.2 us; the launch traced here: 12 us
  starting transfers between devices  7.62 us (62%)
  waiting for transfers between devices  2.27 us (19%)
  Pallas kernels  2.06 us (17%)
    ppermute x6, starting transfers between devices, shards_small(): moved[axes, k] = lax.ppermute(own, axes, [(i, i ^ k) for i in range(size)])  7.62 us
    ppermute x6, waiting for transfers between devices, shards_small(): moved[axes, k] = lax.ppermute(own, axes, [(i, i ^ k) for i in range(size)])  2.27 us
    pallas_call x1, Pallas kernels, shards_small(): pl.pallas_call(functools.partial(pair_kernel, n_cs, n_row), out_shape=jax...  1.11 us
    pallas_call x1, Pallas kernels, pack(): pl.pallas_call(pack_kernel, out_shape=(jax.ShapeDtypeStruct(shape, jnp.bf...  0.94 us
  transfers between devices with their start and end apart: 6, of which 2 were waited for; matrix products, arithmetic and copies ran while one was open for 0% of the time, Pallas kernels for 0%

profile of v2, /device:TPU:0, one launch (start us, length us, event | category | flops | bytes accessed | tf_op | source)
XLA Modules:
  0.0 12.0 jit_solution(3834352100413757941)
XLA Ops:
  0.0 0.9 %pack.1 = (bf16[9,4,256]{2,1,0:T(4,128)(2,1)S(1)}, bf16[2,80,256]{2,1,0:T(8,128)(2,1)S(1)}) custom-call(bf16[4,3,2,256]{3,2,1,0:T(2,128)(2,1)} %spectra_hbm.1, s32[4,3]{1,0:T(4,128)} %mask_hbm.1, bf16[2,80,256]{2,1,0:T(8,128)(2,1)} %constant.2.clone.table_hbm), custom_call_target="tpu_custom_call" | custom-call | tf_op jit(solution)/shard_map/pack/pallas_call | solution.py:62
  1.0 5.1 %collective-permute-start.5 = (bf16[9,4,256]{2,1,0:T(4,128)(2,1)S(1)}, bf16[9,4,256]{2,1,0:T(4,128)(2,1)S(1)}, u32[]{:S(2)}, u32[]{:S(2)}) collective-permute-start(bf16[9,4,256]{2,1,0:T(4,128)(2,1)S(1)} %get-tuple-element.7.refs_0_), channel_id=1, source_target_pairs={{0,12},{4,8},{8,4},{12,0},{1,13},{5,9},{9,5},{13,1},{2,14},{6,10},... | collective-permute-start | bytes 55304 | tf_op jit(solution)/shard_map/ppermute | solution.py:158
  6.1 0.0 collective-permute-start.4
  6.1 0.6 %collective-permute-start.3 = (bf16[9,4,256]{2,1,0:T(4,128)(2,1)S(1)}, bf16[9,4,256]{2,1,0:T(4,128)(2,1)S(1)}, u32[]{:S(2)}, u32[]{:S(2)}) collective-permute-start(bf16[9,4,256]{2,1,0:T(4,128)(2,1)S(1)} %get-tuple-element.7.refs_0_), channel_id=1, source_target_pairs={{0,4},{4,0},{8,12},{12,8},{1,5},{5,1},{9,13},{13,9},{2,6},{6,2},{1... | collective-permute-start | bytes 55304 | tf_op jit(solution)/shard_map/ppermute | solution.py:158
  6.7 0.4 %collective-permute-start.2 = (bf16[9,4,256]{2,1,0:T(4,128)(2,1)S(1)}, bf16[9,4,256]{2,1,0:T(4,128)(2,1)S(1)}, u32[]{:S(2)}, u32[]{:S(2)}) collective-permute-start(bf16[9,4,256]{2,1,0:T(4,128)(2,1)S(1)} %get-tuple-element.7.refs_0_), channel_id=1, source_target_pairs={{0,3},{1,2},{2,1},{3,0},{4,7},{5,6},{6,5},{7,4},{8,11},{9,10},{10,... | collective-permute-start | bytes 55304 | tf_op jit(solution)/shard_map/ppermute | solution.py:158
  7.1 1.3 %collective-permute-start.1 = (bf16[9,4,256]{2,1,0:T(4,128)(2,1)S(1)}, bf16[9,4,256]{2,1,0:T(4,128)(2,1)S(1)}, u32[]{:S(2)}, u32[]{:S(2)}) collective-permute-start(bf16[9,4,256]{2,1,0:T(4,128)(2,1)S(1)} %get-tuple-element.7.refs_0_), channel_id=1, source_target_pairs={{0,2},{1,3},{2,0},{3,1},{4,6},{5,7},{6,4},{7,5},{8,10},{9,11},{10,... | collective-permute-start | bytes 55304 | tf_op jit(solution)/shard_map/ppermute | solution.py:158
  8.4 0.0 collective-permute-done.5.refs_6_
  8.4 0.2 %collective-permute-start = (bf16[9,4,256]{2,1,0:T(4,128)(2,1)S(1)}, bf16[9,4,256]{2,1,0:T(4,128)(2,1)S(1)}, u32[]{:S(2)}, u32[]{:S(2)}) collective-permute-start(bf16[9,4,256]{2,1,0:T(4,128)(2,1)S(1)} %get-tuple-element.7.refs_0_), channel_id=1, source_target_pairs={{0,1},{1,0},{2,3},{3,2},{4,5},{5,4},{6,7},{7,6},{8,9},{9,8},{10,11... | collective-permute-start | bytes 55304 | tf_op jit(solution)/shard_map/ppermute | solution.py:158
  8.6 2.2 %collective-permute-done.4.refs_5_ = bf16[9,4,256]{2,1,0:T(4,128)(2,1)S(1)} collective-permute-done((bf16[9,4,256]{2,1,0:T(4,128)(2,1)S(1)}, bf16[9,4,256]{2,1,0:T(4,128)(2,1)S(1)}, u32[]{:S(2)}, u32[]{:S(2)}) %collective-permute-start.4) | collective-permute-done | bytes 18464 | tf_op jit(solution)/shard_map/ppermute | solution.py:158
  10.7 0.0 collective-permute-done.3.refs_4_
  10.7 0.0 collective-permute-done.2.refs_3_
  10.7 0.1 collective-permute-done.1.refs_2_
  10.8 0.0 collective-permute-done.refs_1_
  10.8 1.1 %pairs.1 = f32[1,16,16]{2,1,0:T(8,128)} custom-call(bf16[9,4,256]{2,1,0:T(4,128)(2,1)S(1)} %get-tuple-element.7.refs_0_, bf16[9,4,256]{2,1,0:T(4,128)(2,1)S(1)} %collective-permute-done.refs_1_, bf16[9,4,256]{2,1,0:T(4,128)(2,1)S(1)} %collective-permute-done.1.refs_2_, bf16[9,4,256]{2,1,0:T(4,128)(2,1)S(1)} %collective-permute-done.2.refs_3_, ...), custom_call_target="tpu_custom_call" | custom-call | tf_op jit(solution)/shard_map/pairs/pallas_call | solution.py:161
Async XLA Ops:
  1.0 7.4 %collective-permute-start.5 = (bf16[9,4,256]{2,1,0:T(4,128)(2,1)S(1)}, bf16[9,4,256]{2,1,0:T(4,128)(2,1)S(1)}, u32[]{:S(2)}, u32[]{:S(2)}) collective-permute-start(bf16[9,4,256]{2,1,0:T(4,128)(2,1)S(1)} %get-tuple-element.7.refs_0_), channel_id=1, source_target_pairs={{0,12},{4,8},{8,4},{12,0},{1,13},{5,9},{9,5},{13,1},{2,14},{6,10},... | collective-permute-start | bytes 55304 | tf_op jit(solution)/shard_map/ppermute | solution.py:158
  6.1 4.7 %collective-permute-start.4 = (bf16[9,4,256]{2,1,0:T(4,128)(2,1)S(1)}, bf16[9,4,256]{2,1,0:T(4,128)(2,1)S(1)}, u32[]{:S(2)}, u32[]{:S(2)}) collective-permute-start(bf16[9,4,256]{2,1,0:T(4,128)(2,1)S(1)} %get-tuple-element.7.refs_0_), channel_id=1, source_target_pairs={{0,8},{4,12},{8,0},{12,4},{1,9},{5,13},{9,1},{13,5},{2,10},{6,14},... | collective-permute-start | bytes 55304 | tf_op jit(solution)/shard_map/ppermute | solution.py:158
  6.1 4.7 %collective-permute-start.3 = (bf16[9,4,256]{2,1,0:T(4,128)(2,1)S(1)}, bf16[9,4,256]{2,1,0:T(4,128)(2,1)S(1)}, u32[]{:S(2)}, u32[]{:S(2)}) collective-permute-start(bf16[9,4,256]{2,1,0:T(4,128)(2,1)S(1)} %get-tuple-element.7.refs_0_), channel_id=1, source_target_pairs={{0,4},{4,0},{8,12},{12,8},{1,5},{5,1},{9,13},{13,9},{2,6},{6,2},{1... | collective-permute-start | bytes 55304 | tf_op jit(solution)/shard_map/ppermute | solution.py:158
  6.7 4.0 %collective-permute-start.2 = (bf16[9,4,256]{2,1,0:T(4,128)(2,1)S(1)}, bf16[9,4,256]{2,1,0:T(4,128)(2,1)S(1)}, u32[]{:S(2)}, u32[]{:S(2)}) collective-permute-start(bf16[9,4,256]{2,1,0:T(4,128)(2,1)S(1)} %get-tuple-element.7.refs_0_), channel_id=1, source_target_pairs={{0,3},{1,2},{2,1},{3,0},{4,7},{5,6},{6,5},{7,4},{8,11},{9,10},{10,... | collective-permute-start | bytes 55304 | tf_op jit(solution)/shard_map/ppermute | solution.py:158
  7.1 3.8 %collective-permute-start.1 = (bf16[9,4,256]{2,1,0:T(4,128)(2,1)S(1)}, bf16[9,4,256]{2,1,0:T(4,128)(2,1)S(1)}, u32[]{:S(2)}, u32[]{:S(2)}) collective-permute-start(bf16[9,4,256]{2,1,0:T(4,128)(2,1)S(1)} %get-tuple-element.7.refs_0_), channel_id=1, source_target_pairs={{0,2},{1,3},{2,0},{3,1},{4,6},{5,7},{6,4},{7,5},{8,10},{9,11},{10,... | collective-permute-start | bytes 55304 | tf_op jit(solution)/shard_map/ppermute | solution.py:158
  8.4 2.5 %collective-permute-start = (bf16[9,4,256]{2,1,0:T(4,128)(2,1)S(1)}, bf16[9,4,256]{2,1,0:T(4,128)(2,1)S(1)}, u32[]{:S(2)}, u32[]{:S(2)}) collective-permute-start(bf16[9,4,256]{2,1,0:T(4,128)(2,1)S(1)} %get-tuple-element.7.refs_0_), channel_id=1, source_target_pairs={{0,1},{1,0},{2,3},{3,2},{4,5},{5,4},{6,7},{7,6},{8,9},{9,8},{10,11... | collective-permute-start | bytes 55304 | tf_op jit(solution)/shard_map/ppermute | solution.py:158
